TPU v7x, 256 devices: a whole 4x4x8 slice. The times are simulated.
256 devices in a mesh: leaf: 16 (over x, y), blk: 16 (over z, core).
Axes of the slice: x: 4, y: 4, z: 8, core: 2. Of those that a mesh axis runs over, the one named last changes fastest.
Arguments:
- near_tiles: bfloat16 [128, 16, 512, 512], P('leaf', 'blk'), may hold values from -0.25 to 0.25
- near_cols: int32 [128, 16], P('leaf', 'blk'), may hold values from 0 to 127, as said below
- near_count: int32 [128], P('leaf'), may hold values from 1 to 16, as said below
- probes: bfloat16 [128, 512, 512], P('leaf'), may hold values from -6 to 6
- mixing: float32 [512, 64], replicated, may hold values from -0.25 to 0.25
- far_tiles: bfloat16 [128, 16, 512, 512], P('leaf', 'blk'), may hold values from -6 to 6
- far_cols: int32 [128, 16], P('leaf', 'blk'), may hold values from 0 to 127, as said below
Outputs:
- coupling: float32 [128, 16, 64, 64], P('leaf', 'blk')
- root_part: float32 [128, 64, 64], P('leaf')
Inputs may be any that keep to these rules, and one draw needn't show every extreme that they name: near_cols[r, k] lies within 8 of r; the slots below near_count[r] name distinct clusters. Slots at or past near_count[r] hold arbitrary tiles that must be ignored. far_cols[r, j] differs from r by more than 8.
All inputs are finite; a program needn't handle non-finite values.
Results may differ from a plain program's by a relative error of at most 0.0041.
Values may be sent and summed in bfloat16 or wider, within the bound.
No kernel may reach another device: no remote copies, remote signals or barrier semaphores. Data moves between devices by JAX's collectives and lax.ppermute only.
A program may use at most 128 MiB of HBM per device.

v0:
```python
import math
import jax
import jax.numpy as jnp
from jax import lax
from jax.sharding import PartitionSpec as P

RANK = 64
REACH = 8
highest = lax.Precision.HIGHEST


def padded(value, sides, width):
    for axis, dim in sides:
        peers, length = (lax.axis_size(axis), value.shape[dim])
        up = [(i, (i + 1) % peers) for i in range(peers - 1)]
        down = [(j, i) for i, j in up]
        last = lax.slice_in_dim(value, length - width, length, axis=dim)
        leading = lax.slice_in_dim(value, 0, width, axis=dim)
        before = lax.ppermute(last, axis, up)
        after = lax.ppermute(leading, axis, down)
        value = jnp.concatenate([before, value, after], axis=dim)
    return value


def partner_2(block, axis, apart):
    count = lax.axis_size(axis)
    route = []
    for low in range(count):
        high = low | 1 << apart
        if high != low and high < count:
            route += [(low, high), (high, low)]
    return lax.ppermute(block, axis, route)


def basis_from(gram_matrix, mixed_rows):
    lower_factor = jnp.linalg.cholesky(gram_matrix)
    solved = jax.scipy.linalg.solve_triangular(
        lower_factor, jnp.swapaxes(mixed_rows, -1, -2), lower=True
    )
    return jnp.swapaxes(solved, -1, -2)


def merge(stacked, mixing):
    mixed_rows = jnp.einsum("...mp,pk->...mk", stacked, mixing, precision=highest)
    gram_matrix = jnp.einsum("...mk,...ml->...kl", mixed_rows, mixed_rows, precision=highest)
    transfer = basis_from(gram_matrix, mixed_rows)
    merged = jnp.einsum("...mk,...mp->...kp", transfer, stacked, precision=highest)
    return (transfer, merged)


def shards(near_tiles, near_cols, near_count, probes, mixing, far_tiles, far_cols):
    local_rows = probes.shape[0]
    near_dev = near_tiles.shape[1]
    leaf_pos = lax.axis_index("leaf")
    blk_pos = lax.axis_index("blk")
    subtrees = lax.axis_size("leaf")
    clusters = local_rows * subtrees
    first_cluster = leaf_pos * local_rows - REACH
    window = padded(probes, (("leaf", 0),), REACH)

    def leaf_sketch(row_index):
        running = jnp.zeros((probes.shape[1], probes.shape[2]), jnp.float32)
        column = near_cols[row_index, 0] - first_cluster
        probe_block = lax.dynamic_index_in_dim(window, column, 0, keepdims=False)
        near_tile = near_tiles[row_index, 0]
        is_live = blk_pos * near_dev + 0 < near_count[row_index]
        running = lax.cond(
            is_live,
            lambda current: jnp.dot(near_tile, probe_block, preferred_element_type=jnp.float32),
            lambda current: current,
            running,
        )
        return running

    partial_sketch = lax.map(leaf_sketch, jnp.arange(local_rows))
    sketch_rows = lax.psum_scatter(partial_sketch, "blk", scatter_dimension=1, tiled=True)
    mixed_rows = jnp.einsum("rbp,pk->rbk", sketch_rows, mixing, precision=highest)
    gram_part = jnp.einsum("rbk,rbl->rkl", mixed_rows, mixed_rows, precision=highest)
    gram_matrix = lax.psum(gram_part, "blk")
    basis_part = basis_from(gram_matrix, mixed_rows)
    proj_part = jnp.einsum("rbk,rbp->rkp", basis_part, sketch_rows, precision=highest)
    leaf_proj = lax.psum(proj_part, "blk")
    basis_low = lax.all_gather(basis_part.astype(jnp.bfloat16), "blk", axis=1, tiled=True)
    all_bases = lax.all_gather(basis_low, "leaf", axis=0, tiled=True)
    far_basis = all_bases[far_cols]
    far_image = jnp.einsum(
        "rjab,rjbk->rjak", far_tiles, far_basis, preferred_element_type=jnp.float32
    )
    coupling = jnp.einsum(
        "rak,rjal->rjkl", basis_low.astype(jnp.float32), far_image, precision=highest
    )
    sub_stack = leaf_proj.reshape(local_rows * RANK, leaf_proj.shape[2])
    sub_transfer, node_sketch = merge(sub_stack, mixing)
    levels = subtrees.bit_length() - 1
    path_factor = jnp.eye(RANK, dtype=jnp.float32)
    for depth_index in range(levels):
        partner = partner_2(node_sketch.astype(jnp.bfloat16), "leaf", depth_index).astype(
            node_sketch.dtype
        )
        is_upper = leaf_pos >> depth_index & 1
        lower_half = jnp.where(is_upper == 1, partner, node_sketch)
        upper_half = jnp.where(is_upper == 1, node_sketch, partner)
        transfer, node_sketch = merge(jnp.concatenate([lower_half, upper_half], 0), mixing)
        picked = lax.dynamic_slice_in_dim(transfer, is_upper * RANK, RANK, 0)
        path_factor = jnp.dot(path_factor, picked, precision=highest)
    sub_blocks = sub_transfer.reshape(local_rows, RANK, RANK)
    root_part = jnp.einsum("cab,bd->cad", sub_blocks, path_factor, precision=highest)
    root_part = root_part * math.sqrt(clusters * RANK)
    return (coupling, root_part)


def solution(mesh):
    in_specs = (
        P("leaf", "blk", None, None),
        P("leaf", "blk"),
        P("leaf"),
        P("leaf", None, None),
        P(),
        P("leaf", "blk", None, None),
        P("leaf", "blk"),
    )
    out_specs = (P("leaf", "blk", None, None), P("leaf", None, None))
    return jax.shard_map(shards, mesh=mesh, in_specs=in_specs, out_specs=out_specs, check_vma=False)
```

profile of v0, /device:TPU:22, one launch (start us, length us, event | category | flops | bytes accessed | tf_op | source)
XLA Modules:
  0.0 679.8 jit_solution(7134080984132930772)
XLA Ops:
  13.1 88.6 %collective-permute-done = bf16[8,512,512]{2,1,0:T(8,128)(2,1)} collective-permute-done((bf16[8,512,512]{2,1,0:T(8,128)(2,1)}, bf16[8,512,512]{2,1,0:T(8,128)(2,1)}, u32[]{:S(2)}, u32[]{:S(2)}) %collective-permute-start) | collective-permute-done | bytes 4194336 | tf_op jit(solution)/shard_map/ppermute | solution.py:19
  104.7 10.8 %pad_maximum_fusion = bf16[24,512,512]{2,1,0:T(8,128)(2,1)} fusion(bf16[8,512,512]{2,1,0:T(8,128)(2,1)} %collective-permute-done.1, bf16[8,512,512]{2,1,0:T(8,128)(2,1)} %param.17, bf16[8,512,512]{2,1,0:T(8,128)(2,1)} %collective-permute-done), kind=kLoop, calls=%fused_computation.9 | loop fusion | flops 12582912 | bytes 25165824 | tf_op jit(solution)/shard_map/concatenate | solution.py:21
  115.4 60.4 %while.10 = (s32[]{:T(128)}, f32[8,512,512]{2,1,0:T(8,128)}, s32[8]{0:T(128)S(1)}, s32[8]{0:T(128)S(1)}, s32[]{:T(128)}, /*index=5*/bf16[8,1,512,512]{3,2,1,0:T(...) while((s32[]{:T(128)}, f32[8,512,512]{2,1,0:T(8,128)}, ...), condition=%wide.region_3.4_spmd, body=%wide.region_0.3_spmd.sunk | while | flops 268435456 | bytes 4195627 | solution.py:75
  175.9 75.0 %reduce-scatter.2.cloned.1.call-done = f32[8,32,512]{2,1,0:T(8,128)} async-done(((f32[8,512,512]{2,1,0:T(8,128)}), f32[8,32,512]{2,1,0:T(8,128)}) %reduce-scatter.2.cloned.1.call-update) | async-done | bytes 524304 | tf_op jit(solution)/shard_map/reduce_scatter | solution.py:76
  253.9 108.8 %all-reduce.3.cloned.1.call-done = f32[8,64,64]{1,2,0:T(8,128)} async-done(((f32[8,64,64]{1,2,0:T(8,128)}), f32[8,64,64]{1,2,0:T(8,128)}) %all-reduce.3.cloned.1.call-update) | async-done | bytes 131088 | tf_op jit(solution)/shard_map/psum | solution.py:79
  364.8 46.9 %custom-call.17 = f32[8,64,64]{2,1,0:T(8,128)S(1)} custom-call(f32[8,64,64]{2,1,0:T(8,128)S(1)} %fusion.13), custom_call_target="Cholesky" | custom-call | tf_op jit(solution)/shard_map/jit(cholesky)/cholesky | solution.py:36
  411.9 39.3 %custom-call.18 = f32[8,1,64,64]{2,3,1,0:T(8,128)S(1)} custom-call(f32[8,1,64,64]{3,2,1,0:T(8,128)S(1)} %select_bitcast_fusion), custom_call_target="InvertDiagBlocksLowerTriangular" | custom-call | tf_op jit(solution)/shard_map/jit(_solve_triangular)/vmap()/triangular_solve | solution.py:37
  454.9 18.4 %all_gather.6 = bf16[8,512,64]{2,1,0:T(8,128)(2,1)S(1)} all-gather(bf16[8,32,64]{2,1,0:T(8,128)(2,1)S(1)} %convert_bitcast_fusion), channel_id=1, replica_groups=mesh['leaf'=16,'blk'=16] {'blk'}, dimensions={1}, use_global_device_ids=true | all-gather | bytes 557056 | tf_op jit(solution)/shard_map/all_gather | solution.py:83
  474.5 93.2 %all-reduce.5.cloned.1.call-done = f32[512,512]{1,0:T(8,128)} async-done(((f32[512,512]{1,0:T(8,128)}), f32[512,512]{1,0:T(8,128)}) %all-reduce.5.cloned.1.call-update) | async-done | bytes 1048592 | tf_op jit(solution)/shard_map/psum | solution.py:82
  570.5 5.8 cholesky.127
  577.7 4.9 custom-call.19
  586.5 4.7 collective-permute-done.2
  591.9 5.8 cholesky.138
  599.1 4.9 custom-call.23
  605.3 5.9 collective-permute-done.3
  611.9 5.8 cholesky.149
  619.1 4.9 custom-call.24
  625.4 5.0 collective-permute-done.4
  631.1 5.8 cholesky.160
  638.3 4.9 custom-call.25
  645.6 4.3 collective-permute-done.5
  650.5 5.8 cholesky.171
  657.7 4.9 custom-call.26
  664.2 4.0 gather_fusion
  (146 shorter events, 105.0 us)
Async XLA Ops:
  7.2 243.7 %copy-start = (f32[512,64]{0,1:T(8,128)S(1)}, f32[512,64]{0,1:T(8,128)}, u32[]{:S(2)}) copy-start(f32[512,64]{0,1:T(8,128)} %param.18) | copy-start | bytes 393220
  7.2 243.7 %reduce-scatter.2.cloned.1.call-start = ((), (), s32[]{:S(2)}) async-start(), calls=%async_computation.1 | async-start | bytes 8912896 | tf_op jit(solution)/shard_map/reduce_scatter | solution.py:76
  7.2 94.5 %collective-permute-start = (bf16[8,512,512]{2,1,0:T(8,128)(2,1)}, bf16[8,512,512]{2,1,0:T(8,128)(2,1)}, u32[]{:S(2)}, u32[]{:S(2)}) collective-permute-start(bf16[8,512,512]{2,1,0:T(8,128)(2,1)} %param.17), channel_id=1, source_target_pairs={{0,16},{16,32},{32,48},{48,64},{64,80},{80,96},{96,112},{112,128},... | collective-permute-start | bytes 12582920 | tf_op jit(solution)/shard_map/ppermute | solution.py:19
  10.4 94.2 %collective-permute-start.1 = (bf16[8,512,512]{2,1,0:T(8,128)(2,1)}, bf16[8,512,512]{2,1,0:T(8,128)(2,1)}, u32[]{:S(2)}, u32[]{:S(2)}) collective-permute-start(bf16[8,512,512]{2,1,0:T(8,128)(2,1)} %param.17), channel_id=1, source_target_pairs={{16,0},{32,16},{48,32},{64,48},{80,64},{96,80},{112,96},{128,112},... | collective-permute-start | bytes 12582920 | tf_op jit(solution)/shard_map/ppermute | solution.py:20
  13.1 102.3 %copy-start.1 = (s32[8]{0:T(128)S(1)}, s32[8]{0:T(128)}, u32[]{:S(2)}) copy-start(s32[8]{0:T(128)} %param.16) | copy-start | bytes 100
  13.1 102.3 %copy-start.2 = (s32[8,1]{0,1:T(1,128)S(1)}, s32[8,1]{0,1:T(1,128)}, u32[]{:S(2)}) copy-start(s32[8,1]{0,1:T(1,128)} %param.15) | copy-start | bytes 100
  175.8 298.7 %copy-start.3 = (s32[8,1]{0,1:T(1,128)S(1)}, s32[8,1]{0,1:T(1,128)}, u32[]{:S(2)}) copy-start(s32[8,1]{0,1:T(1,128)} %param.20) | copy-start | bytes 100
  175.8 186.9 %all-reduce.3.cloned.1.call-start = ((), (), s32[]{:S(2)}) async-start(), calls=%async_computation.2 | async-start | bytes 524288 | tf_op jit(solution)/shard_map/psum | solution.py:79
  253.8 314.0 %all-reduce.5.cloned.1.call-start = ((), (), s32[]{:S(2)}) async-start(), calls=%async_computation.4 | async-start | bytes 2097152 | tf_op jit(solution)/shard_map/psum | solution.py:82
  454.8 209.4 %all-gather.2.cloned.1.call-start = ((), (), s32[]{:S(2)}) async-start(), calls=%async_computation.3 | async-start | bytes 8912896 | tf_op jit(solution)/shard_map/all_gather | solution.py:84
  584.9 6.3 collective-permute-start.2
  604.5 6.7 collective-permute-start.3
  624.5 5.9 collective-permute-start.4
  643.7 6.1 collective-permute-start.5
Sparse Core Ops, SparseCore 0:
  175.9 74.8 reduce-scatter.1
  253.9 108.7 all-reduce.2
  454.9 112.7 all-reduce.4
  570.0 76.4 all-gather.1
where the time goes:
time: 681 us; the launch traced here: 680 us
  waiting for transfers between devices  388 us (57%)
  other arithmetic  159 us (23%)
  matrix products  35 us (5%)
  local copies, waits for them, and re-layouts  30.2 us (4%)
  loops' own time  24.6 us (4%)
  blocking collectives  18.4 us (3%)
  between operations  14.2 us (2%)
  starting transfers between devices  10.2 us (1%)
    psum x1, waiting for transfers between devices, shards(): gram_matrix = lax.psum(gram_part, 'blk')  109 us
    psum x1, waiting for transfers between devices, shards(): leaf_proj = lax.psum(proj_part, 'blk')  93.2 us
    ppermute x1, waiting for transfers between devices, padded(): before = lax.ppermute(last, axis, up)  88.6 us
    another operation x19, other arithmetic, basis_from(): lower_factor = jnp.linalg.cholesky(gram_matrix)  79.7 us
    reduce_scatter x1, waiting for transfers between devices, shards(): lax.psum_scatter(partial_sketch, 'blk', scatter_dimension=1, tiled=True)  75 us
    another operation x13, other arithmetic, basis_from(): jax.scipy.linalg.solve_triangular(lower_factor, jnp.swapaxes(mixed_rows,...  67.2 us
    another operation x1, loops' own time, shards(): partial_sketch = lax.map(leaf_sketch, jnp.arange(local_rows))  19.8 us
    ppermute x4, waiting for transfers between devices, partner_2(): return lax.ppermute(block, axis, route)  19.7 us
  transfers between devices with their start and end apart: 10, of which 9 were waited for; matrix products, arithmetic and copies ran while one was open for 11% of the time, Pallas kernels for 0%

commit v1 on v0

--- a/solution.py
+++ b/solution.py
@@ -79,7 +79,11 @@
     gram_matrix = lax.psum(gram_part, "blk")
     basis_part = basis_from(gram_matrix, mixed_rows)
     proj_part = jnp.einsum("rbk,rbp->rkp", basis_part, sketch_rows, precision=highest)
-    leaf_proj = lax.psum(proj_part, "blk")
+    leaf_proj = proj_part
+    for hop in (1, 2, 4, 8):
+        leaf_proj = leaf_proj + lax.ppermute(
+            leaf_proj, "blk", [(dev, dev ^ hop) for dev in range(16)]
+        )
     basis_low = lax.all_gather(basis_part.astype(jnp.bfloat16), "blk", axis=1, tiled=True)
     all_bases = lax.all_gather(basis_low, "leaf", axis=0, tiled=True)
     far_basis = all_bases[far_cols]

time: 681 us -> 710 us (1.043)
  waiting for transfers between devices: 388 us -> 410 us
  starting transfers between devices: 10.2 us -> 18.8 us
    ppermute x0 -> x4, waiting for transfers between devices: none -> 120 us  [shards(): lax.ppermute(leaf_proj, 'blk', [(dev, dev ^ hop) for dev in range(16)])]
    psum x1 -> x0, waiting for transfers between devices: 93.2 us -> none  [shards(): leaf_proj = lax.psum(proj_part, 'blk')]
    ppermute x0 -> x4, starting transfers between devices: none -> 8.18 us  [shards(): lax.ppermute(leaf_proj, 'blk', [(dev, dev ^ hop) for dev in range(16)])]
  transfers between devices with their start and end apart: 10 -> 13, of which waited for: 9 -> 12; matrix products, arithmetic and copies ran while one was open for 11% -> 10% of each run, Pallas kernels for 0% -> 0%
where the time goes in v1:
time: 710 us; the launch traced here: 709 us
  waiting for transfers between devices  410 us (58%)
  other arithmetic  161 us (23%)
  matrix products  31.4 us (4%)
  local copies, waits for them, and re-layouts  30.2 us (4%)
  loops' own time  24.6 us (3%)
  starting transfers between devices  18.8 us (3%)
  blocking collectives  18.4 us (3%)
  between operations  14.2 us (2%)
    ppermute x4, waiting for transfers between devices, shards(): lax.ppermute(leaf_proj, 'blk', [(dev, dev ^ hop) for dev in range(16)])  120 us
    psum x1, waiting for transfers between devices, shards(): gram_matrix = lax.psum(gram_part, 'blk')  109 us
    ppermute x1, waiting for transfers between devices, padded(): before = lax.ppermute(last, axis, up)  88.6 us
    another operation x19, other arithmetic, basis_from(): lower_factor = jnp.linalg.cholesky(gram_matrix)  79.7 us
    reduce_scatter x1, waiting for transfers between devices, shards(): lax.psum_scatter(partial_sketch, 'blk', scatter_dimension=1, tiled=True)  75 us
    another operation x13, other arithmetic, basis_from(): jax.scipy.linalg.solve_triangular(lower_factor, jnp.swapaxes(mixed_rows,...  67.2 us
    another operation x1, loops' own time, shards(): partial_sketch = lax.map(leaf_sketch, jnp.arange(local_rows))  19.8 us
    all_gather x1, blocking collectives, shards(): lax.all_gather(basis_part.astype(jnp.bfloat16), 'blk', axis=1, tiled=True)  18.4 us
  transfers between devices with their start and end apart: 13, of which 12 were waited for; matrix products, arithmetic and copies ran while one was open for 10% of the time, Pallas kernels for 0%

profile of v1, /device:TPU:22, one launch (start us, length us, event | category | flops | bytes accessed | tf_op | source)
XLA Modules:
  0.0 708.6 jit_solution(5096418935061471566)
XLA Ops:
  13.1 88.6 %collective-permute-done = bf16[8,512,512]{2,1,0:T(8,128)(2,1)} collective-permute-done((bf16[8,512,512]{2,1,0:T(8,128)(2,1)}, bf16[8,512,512]{2,1,0:T(8,128)(2,1)}, u32[]{:S(2)}, u32[]{:S(2)}) %collective-permute-start) | collective-permute-done | bytes 4194336 | tf_op jit(solution)/shard_map/ppermute | solution.py:19
  104.7 10.8 %pad_maximum_fusion = bf16[24,512,512]{2,1,0:T(8,128)(2,1)} fusion(bf16[8,512,512]{2,1,0:T(8,128)(2,1)} %collective-permute-done.1, bf16[8,512,512]{2,1,0:T(8,128)(2,1)} %param.17, bf16[8,512,512]{2,1,0:T(8,128)(2,1)} %collective-permute-done), kind=kLoop, calls=%fused_computation.9 | loop fusion | flops 12582912 | bytes 25165824 | tf_op jit(solution)/shard_map/concatenate | solution.py:21
  115.4 60.4 %while.10 = (s32[]{:T(128)}, f32[8,512,512]{2,1,0:T(8,128)}, s32[8]{0:T(128)S(1)}, s32[8]{0:T(128)S(1)}, s32[]{:T(128)}, /*index=5*/bf16[8,1,512,512]{3,2,1,0:T(...) while((s32[]{:T(128)}, f32[8,512,512]{2,1,0:T(8,128)}, ...), condition=%wide.region_3.4_spmd, body=%wide.region_0.3_spmd.sunk | while | flops 268435456 | bytes 4195627 | solution.py:75
  175.9 75.0 %reduce-scatter.2.cloned.1.call-done = f32[8,32,512]{2,1,0:T(8,128)} async-done(((f32[8,512,512]{2,1,0:T(8,128)}), f32[8,32,512]{2,1,0:T(8,128)}) %reduce-scatter.2.cloned.1.call-update) | async-done | bytes 524304 | tf_op jit(solution)/shard_map/reduce_scatter | solution.py:76
  253.9 108.8 %all-reduce.2.cloned.1.call-done = f32[8,64,64]{1,2,0:T(8,128)} async-done(((f32[8,64,64]{1,2,0:T(8,128)}), f32[8,64,64]{1,2,0:T(8,128)}) %all-reduce.2.cloned.1.call-update) | async-done | bytes 131088 | tf_op jit(solution)/shard_map/psum | solution.py:79
  364.8 46.9 %custom-call.17 = f32[8,64,64]{2,1,0:T(8,128)S(1)} custom-call(f32[8,64,64]{2,1,0:T(8,128)S(1)} %fusion.13), custom_call_target="Cholesky" | custom-call | tf_op jit(solution)/shard_map/jit(cholesky)/cholesky | solution.py:36
  412.0 39.3 %custom-call.18 = f32[8,1,64,64]{2,3,1,0:T(8,128)S(1)} custom-call(f32[8,1,64,64]{3,2,1,0:T(8,128)S(1)} %select_bitcast_fusion), custom_call_target="InvertDiagBlocksLowerTriangular" | custom-call | tf_op jit(solution)/shard_map/jit(_solve_triangular)/vmap()/triangular_solve | solution.py:37
  451.7 18.4 %all_gather.6 = bf16[8,512,64]{2,1,0:T(8,128)(2,1)S(1)} all-gather(bf16[8,32,64]{2,1,0:T(8,128)(2,1)S(1)} %convert_bitcast_fusion), channel_id=1, replica_groups=mesh['leaf'=16,'blk'=16] {'blk'}, dimensions={1}, use_global_device_ids=true | all-gather | bytes 557056 | tf_op jit(solution)/shard_map/all_gather | solution.py:87
  477.1 24.6 %collective-permute-done.3 = f32[8,64,512]{2,1,0:T(8,128)S(1)} collective-permute-done((f32[8,64,512]{2,1,0:T(8,128)S(1)}, f32[8,64,512]{2,1,0:T(8,128)S(1)}, u32[]{:S(2)}, u32[]{:S(2)}) %collective-permute-start.3) | collective-permute-done | bytes 1048608 | tf_op jit(solution)/shard_map/ppermute | solution.py:84
  503.8 46.1 %collective-permute-done.4 = f32[8,64,512]{2,1,0:T(8,128)S(1)} collective-permute-done((f32[8,64,512]{2,1,0:T(8,128)S(1)}, f32[8,64,512]{2,1,0:T(8,128)S(1)}, u32[]{:S(2)}, u32[]{:S(2)}) %collective-permute-start.4) | collective-permute-done | bytes 1048608 | tf_op jit(solution)/shard_map/ppermute | solution.py:84
  550.1 4.9 collective-permute-start.5
  555.1 46.8 %collective-permute-done.5 = f32[8,64,512]{2,1,0:T(8,128)} collective-permute-done((f32[8,64,512]{2,1,0:T(8,128)S(1)}, f32[8,64,512]{2,1,0:T(8,128)}, u32[]{:S(2)}, u32[]{:S(2)}) %collective-permute-start.5) | collective-permute-done | bytes 1048608 | tf_op jit(solution)/shard_map/ppermute | solution.py:84
  604.9 5.8 cholesky.127
  612.0 4.9 custom-call.19
  623.1 5.8 cholesky.138
  630.3 4.9 custom-call.23
  636.6 5.0 collective-permute-done.7
  642.3 5.8 cholesky.149
  649.5 4.9 custom-call.24
  660.2 5.8 cholesky.160
  667.4 4.9 custom-call.25
  674.6 4.0 collective-permute-done.9
  679.4 5.8 cholesky.171
  686.6 4.9 custom-call.26
  (155 shorter events, 119.3 us)
Async XLA Ops:
  7.2 243.7 %copy-start = (f32[512,64]{0,1:T(8,128)S(1)}, f32[512,64]{0,1:T(8,128)}, u32[]{:S(2)}) copy-start(f32[512,64]{0,1:T(8,128)} %param.18) | copy-start | bytes 393220
  7.2 243.7 %reduce-scatter.2.cloned.1.call-start = ((), (), s32[]{:S(2)}) async-start(), calls=%async_computation.1 | async-start | bytes 8912896 | tf_op jit(solution)/shard_map/reduce_scatter | solution.py:76
  7.2 94.5 %collective-permute-start = (bf16[8,512,512]{2,1,0:T(8,128)(2,1)}, bf16[8,512,512]{2,1,0:T(8,128)(2,1)}, u32[]{:S(2)}, u32[]{:S(2)}) collective-permute-start(bf16[8,512,512]{2,1,0:T(8,128)(2,1)} %param.17), channel_id=1, source_target_pairs={{0,16},{16,32},{32,48},{48,64},{64,80},{80,96},{96,112},{112,128},... | collective-permute-start | bytes 12582920 | tf_op jit(solution)/shard_map/ppermute | solution.py:19
  10.4 94.2 %collective-permute-start.1 = (bf16[8,512,512]{2,1,0:T(8,128)(2,1)}, bf16[8,512,512]{2,1,0:T(8,128)(2,1)}, u32[]{:S(2)}, u32[]{:S(2)}) collective-permute-start(bf16[8,512,512]{2,1,0:T(8,128)(2,1)} %param.17), channel_id=1, source_target_pairs={{16,0},{32,16},{48,32},{64,48},{80,64},{96,80},{112,96},{128,112},... | collective-permute-start | bytes 12582920 | tf_op jit(solution)/shard_map/ppermute | solution.py:20
  13.1 102.3 %copy-start.1 = (s32[8]{0:T(128)S(1)}, s32[8]{0:T(128)}, u32[]{:S(2)}) copy-start(s32[8]{0:T(128)} %param.16) | copy-start | bytes 100
  13.1 102.3 %copy-start.2 = (s32[8,1]{0,1:T(1,128)S(1)}, s32[8,1]{0,1:T(1,128)}, u32[]{:S(2)}) copy-start(s32[8,1]{0,1:T(1,128)} %param.15) | copy-start | bytes 100
  175.8 186.9 %all-reduce.2.cloned.1.call-start = ((), (), s32[]{:S(2)}) async-start(), calls=%async_computation.2 | async-start | bytes 524288 | tf_op jit(solution)/shard_map/psum | solution.py:79
  253.8 439.3 %all-gather.2.cloned.1.call-start = ((), (), s32[]{:S(2)}) async-start(), calls=%async_computation.3 | async-start | bytes 8912896 | tf_op jit(solution)/shard_map/all_gather | solution.py:88
  363.8 191.3 %copy-start.3 = (s32[8,1]{0,1:T(1,128)S(1)}, s32[8,1]{0,1:T(1,128)}, u32[]{:S(2)}) copy-start(s32[8,1]{0,1:T(1,128)} %param.20) | copy-start | bytes 100
  473.3 2.7 collective-permute-start.2
  476.2 25.5 %collective-permute-start.3 = (f32[8,64,512]{2,1,0:T(8,128)S(1)}, f32[8,64,512]{2,1,0:T(8,128)S(1)}, u32[]{:S(2)}, u32[]{:S(2)}) collective-permute-start(f32[8,64,512]{2,1,0:T(8,128)S(1)} %add.73), channel_id=1, source_target_pairs={{0,2},{1,3},{2,0},{3,1},{4,6},{5,7},{6,4},{7,5},{8,10},{9,11},{10,... | collective-permute-start | bytes 3145736 | tf_op jit(solution)/shard_map/ppermute | solution.py:84
  501.9 48.0 %collective-permute-start.4 = (f32[8,64,512]{2,1,0:T(8,128)S(1)}, f32[8,64,512]{2,1,0:T(8,128)S(1)}, u32[]{:S(2)}, u32[]{:S(2)}) collective-permute-start(f32[8,64,512]{2,1,0:T(8,128)S(1)} %add.74), channel_id=1, source_target_pairs={{0,4},{1,5},{2,6},{3,7},{4,0},{5,1},{6,2},{7,3},{8,12},{9,13},{10,... | collective-permute-start | bytes 3145736 | tf_op jit(solution)/shard_map/ppermute | solution.py:84
  550.1 51.8 %collective-permute-start.5 = (f32[8,64,512]{2,1,0:T(8,128)S(1)}, f32[8,64,512]{2,1,0:T(8,128)}, u32[]{:S(2)}, u32[]{:S(2)}) collective-permute-start(f32[8,64,512]{2,1,0:T(8,128)S(1)} %add.75), channel_id=1, source_target_pairs={{0,8},{1,9},{2,10},{3,11},{4,12},{5,13},{6,14},{7,15},{8,0},{9,1},... | collective-permute-start | bytes 3145736 | tf_op jit(solution)/shard_map/ppermute | solution.py:84
  618.0 4.3 collective-permute-start.6
  635.7 5.9 collective-permute-start.7
  654.9 4.6 collective-permute-start.8
  672.8 5.9 collective-permute-start.9
Sparse Core Ops, SparseCore 0:
  175.9 74.8 reduce-scatter.1
  253.9 108.7 all-reduce.1
  471.3 74.4 all-gather.1
